TPU v7x, 32 devices: a whole 2x2x4 slice. The times are simulated.
32 devices in a mesh: tm: 8 (over y, x, core), space: 4 (over z).
Axes of the slice: x: 2, y: 2, z: 4, core: 2. Of those that a mesh axis runs over, the one named last changes fastest.
Arguments:
- forcing: float32 [256, 32768], P('tm', 'space'), may hold values from -6 to 6
- op_main: bfloat16 [512, 64, 448], P('space'), may hold values from -0.1205 to 2.61
- op_mass: bfloat16 [512, 64, 448], P('space'), may hold values from -0.0401 to 1.045
- jacobi_inv: bfloat16 [512, 64, 64], P('space'), may hold values from -0.0301 to 0.635
Outputs:
- spec_real: float32 [256, 32768], P('tm', 'space')
- spec_imag: float32 [256, 32768], P('tm', 'space')
- time_field: float32 [256, 32768], P('tm', 'space')
All inputs are finite; a program needn't handle non-finite values.
Results may differ from a plain program's by a relative error of at most 0.0058.
Values may be sent and summed in bfloat16 or wider, within the bound.
A program may use at most 128 MiB of HBM per device.

v0:
```python
import functools
import math

import jax
import jax.numpy as jnp
import numpy as np
from jax import lax
from jax.experimental import pallas as pl
from jax.experimental.pallas import tpu as pltpu
from jax.sharding import PartitionSpec as P

BS = 64
BX = 4
BY = 4
LINE = BX * BS

alpha_decay = 0.25
MESH = pl.DeviceIdType.MESH


def split_table(table):
    high = table.astype(jnp.bfloat16)
    low = (table - high.astype(np.float64)).astype(jnp.bfloat16)
    return np.stack([high, low])


def tables(length):
    half = length // 2
    ids = np.arange(length)
    freqs = np.arange(half)
    angles = 2.0 * math.pi * ((freqs[:, None] * ids[None, :]) % length) / length
    norm = 1.0 / math.sqrt(length)
    real_rows = np.cos(angles) * norm
    imag_rows = -np.sin(angles) * norm
    imag_rows[0] = np.where(ids % 2 == 0, norm, -norm)
    packed = np.concatenate([real_rows, imag_rows], axis=0)
    decay = alpha_decay ** (ids / length)
    forward = packed * decay[None, :]
    weight = np.full((length,), 2.0)
    weight[0] = 1.0
    weight[half] = 1.0
    inverse = (packed * weight[:, None]).T / decay[:, None]
    mirror = np.zeros((length, length))
    mirror[0, half] = 1.0
    for row in range(1, half):
        mirror[row, half - row] = 1.0
        mirror[half + row, length - row] = -1.0
    modulus = alpha_decay ** (1.0 / length)
    beta = modulus * np.exp(-2j * math.pi * freqs / length)
    beta_high = beta.real.copy()
    beta_high[0] = -modulus
    beta_cross = beta.imag.copy()
    beta_cross[0] = 0.0
    coefs = np.stack([beta.real, beta_high, beta_cross]).astype(np.float32)
    coefs = np.ascontiguousarray(np.broadcast_to(coefs[:, :, None], (3, half, 128)))
    return split_table(forward), split_table(inverse), mirror.astype(jnp.bfloat16), coefs


def place(rank, count):
    quarter = count // 4
    chip = rank // quarter
    return (chip ^ (chip >> 1)) * quarter + rank % quarter


def dot_nn(left, right):
    return jnp.dot(left, right, preferred_element_type=jnp.float32)


def dot_nt(left, right):
    return lax.dot_general(
        left, right, (((1,), (1,)), ((), ())), preferred_element_type=jnp.float32
    )


def kernel(
    tm, space, lines,
    forcing, op_main, op_mass, jacobi, fwd, inv, mir, coef,
    spec_out, time_out,
    wide, sends, cols, main_raw, mass_raw, jac_raw, pick, picked, picked_jac, fwd_v, inv_v, mir_v, weights, gains,
    field, rhs, first, acc, spec_v, time_v,
    load_sem, main_sem, mass_sem, jac_sem, chunk_sem, own_sem,
    send1, recv1, send2, recv2, send3, recv3, send4, recv4,
):
    bf16 = jnp.bfloat16
    me = lax.axis_index("tm")
    plane = lax.axis_index("space")
    steps = forcing.shape[0]
    length = steps * tm
    half = length // 2
    width = lines * LINE
    blocks = lines * BX
    reach = BY // lines
    total = tm * space
    spot = place(me, tm)
    order = plane * tm + spot
    hops = [d for m in range(1, reach + 1) for d in (m, -m)]

    def coords(position):
        return {"tm": place(lax.rem(position, tm), tm), "space": position // tm}

    chunks = []
    peers = list(range(tm - 1, -1, -1))
    for d in peers:
        begin = pl.multiple_of(place(me ^ d, tm) * width, width)
        copy = pltpu.make_async_copy(
            forcing.at[:, pl.ds(begin, width)], wide.at[d], chunk_sem.at[d]
        )
        copy.start()
        chunks.append(copy)
    groups = BS // 8

    def fetch(source, target, sem, g):
        span = pl.ds(pl.multiple_of(g * 8, 8), 8)
        return pltpu.make_async_copy(source.at[span], target.at[span], sem.at[g])

    loads = [
        pltpu.make_async_copy(fwd, fwd_v, load_sem.at[0]),
        pltpu.make_async_copy(inv, inv_v, load_sem.at[1]),
        pltpu.make_async_copy(mir, mir_v, load_sem.at[2]),
    ]
    for g in range(groups):
        fetch(jacobi, jac_raw, jac_sem, g).start()
    loads[0].start()
    for g in range(groups):
        fetch(op_main, main_raw, main_sem, g).start()
    for g in range(groups):
        fetch(op_mass, mass_raw, mass_sem, g).start()
    loads[1].start()
    loads[2].start()

    barrier = pltpu.get_barrier_semaphore()
    for d in range(1, tm):
        pl.semaphore_signal(barrier, 1, device_id={"tm": me ^ d, "space": plane}, device_id_type=MESH)
    for hop in hops:
        @pl.when(jnp.logical_and(order + hop >= 0, order + hop < total))
        def _():
            pl.semaphore_signal(barrier, 1, device_id=coords(order + hop), device_id_type=MESH)
    others = sum(
        jnp.where(jnp.logical_and(order + hop >= 0, order + hop < total), 1, 0) for hop in hops
    )
    pl.semaphore_wait(barrier, tm - 1 + others)

    row = pl.multiple_of(me * steps, steps)

    def exchange1(d):
        return pltpu.make_async_remote_copy(
            src_ref=sends.at[d], dst_ref=cols.at[pl.ds(row, steps), :],
            send_sem=send1.at[d], recv_sem=recv1.at[d],
            device_id={"tm": me ^ d, "space": plane}, device_id_type=MESH,
        )

    def arrival1(d):
        theirs = pl.multiple_of((me ^ d) * steps, steps)
        return pltpu.make_async_remote_copy(
            src_ref=sends.at[d], dst_ref=cols.at[pl.ds(theirs, steps), :],
            send_sem=send1.at[d], recv_sem=recv1.at[d],
            device_id={"tm": me ^ d, "space": plane}, device_id_type=MESH,
        )

    for d, copy in zip(peers, chunks):
        copy.wait()
        if d == 0:
            cols[pl.ds(row, steps), :] = wide[d].astype(bf16)
        else:
            sends[d] = wide[d].astype(bf16)
            exchange1(d).start()

    held = op_main.shape[2]
    pick_row = lax.broadcasted_iota(jnp.int32, (blocks * 8, 2 * held), 0)
    pick_col = lax.broadcasted_iota(jnp.int32, (blocks * 8, 2 * held), 1)
    late = jnp.where(pick_col >= held, 1, 0)
    same = pick_col - late * held == spot * blocks + pick_row // 8
    for p in range(4):
        hit = jnp.logical_and(same, pick_row % 8 == 2 * p + late)
        pick[p] = jnp.where(hit, 1.0, 0.0).astype(bf16)

    def gather(source, raw, sem, target):
        @pl.loop(0, groups)
        def _(g):
            fetch(source, raw, sem, g).wait()
            value = None
            for p in range(4):
                pair = jnp.concatenate([raw[g * 8 + 2 * p], raw[g * 8 + 2 * p + 1]], axis=1)
                term = dot_nt(pick[p], pair)
                value = term if value is None else value + term
            span = pl.ds(pl.multiple_of(g * 8, 8), 8)
            target[:, span, :] = value.reshape(blocks, 8, value.shape[1])

    zero = jnp.zeros((BS, BS), bf16)
    first_y = lax.rem(spot * lines, BY)

    def assemble(part):
        for i in range(lines):
            for x in range(BX):
                block = i * BX + x
                slot = [picked[block, :, s * BS:(s + 1) * BS].astype(bf16) for s in range(7)]
                span = pl.ds(part * LINE + x * BS, BS)
                along = {x: slot[0], x - 1: slot[1], x + 1: slot[2]}
                weights[i, 0, span, :] = jnp.concatenate(
                    [along.get(j, zero) for j in range(BX)], axis=1
                )
                below, above = slot[3], slot[4]
                if lines != BY:
                    y = first_y + i
                    below = jnp.where(y > 0, below, zero)
                    above = jnp.where(y < BY - 1, above, zero)
                for s, piece in ((1, below), (2, above), (3, slot[5]), (4, slot[6])):
                    weights[i, s, span, :] = jnp.concatenate(
                        [piece if j == x else zero for j in range(BX)], axis=1
                    )

    gather(jacobi, jac_raw, jac_sem, picked_jac)
    for i in range(lines):
        for x in range(BX):
            own = picked_jac[i * BX + x].astype(bf16)
            gains[i, pl.ds(x * BS, BS), :] = jnp.concatenate(
                [own if j == x else zero for j in range(BX)], axis=1
            )
    gather(op_main, main_raw, main_sem, picked)
    assemble(0)

    for hop in hops:
        @pl.when(jnp.logical_or(order - hop < 0, order - hop >= total))
        def _():
            field[pl.ds(BY - hop * lines, lines)] = jnp.zeros((lines, length, LINE), bf16)

    def halo(hop, i, target):
        index = hops.index(hop) * lines + i
        return pltpu.make_async_remote_copy(
            src_ref=field.at[BY + i], dst_ref=field.at[BY - hop * lines + i],
            send_sem=send2.at[index], recv_sem=recv2.at[index],
            device_id=coords(target), device_id_type=MESH,
        )

    loads[0].wait()
    for d in range(1, tm):
        arrival1(d).wait_recv()

    for i in range(lines):
        part = cols[:, i * LINE:(i + 1) * LINE]
        hat = dot_nn(fwd_v[0], part) + dot_nn(fwd_v[1], part)
        rhs[i] = hat
        image = dot_nt(hat.astype(bf16), gains[i])
        first[i] = image
        field[BY + i] = image.astype(bf16)
        for hop in hops:
            @pl.when(jnp.logical_and(order + hop >= 0, order + hop < total))
            def _():
                halo(hop, i, order + hop).start()

    gather(op_mass, mass_raw, mass_sem, picked)
    assemble(1)

    def outside(j):
        return j < 0 or j >= lines

    for i in range(lines):
        value = dot_nt(field[BY + i], weights[i, 0])
        for s, j in ((1, i - 1), (2, i + 1)):
            if not outside(j):
                value += dot_nt(field[BY + j], weights[i, s])
        acc[i] = value

    def arrive(hop, i):
        @pl.when(jnp.logical_and(order - hop >= 0, order - hop < total))
        def _():
            halo(hop, i, order - hop).wait_recv()

    if lines != BY:
        for hop in hops:
            for i in range(lines):
                arrive(hop, i)
    loads[1].wait()
    loads[2].wait()
    top = lax.broadcasted_iota(jnp.int32, (half, LINE), 0) == 0
    own_low = coef[0][:, :1]
    own_high = coef[1][:, :1]
    cross = coef[2][:, :1]
    seconds = []
    for i in range(lines):
        if lines == BY:
            arrive(1, i)
            arrive(-1, i)
        value = acc[i] + dot_nt(field[i], weights[i, 3])
        value += dot_nt(field[i + 2 * BY], weights[i, 4])
        if lines != BY:
            for s, j in ((1, i - 1), (2, i + 1)):
                if outside(j):
                    value += dot_nt(field[BY + j], weights[i, s])
        mass_re = value[:half, LINE:]
        mass_im = value[half:, LINE:]
        res_re = rhs[i, :half] - value[:half, :LINE] + own_low * mass_re - cross * mass_im
        res_im = rhs[i, half:] - value[half:, :LINE] + own_high * mass_im + cross * mass_re
        residue = jnp.concatenate([res_re.astype(bf16), res_im.astype(bf16)], axis=0)
        second = first[i] + dot_nt(residue, gains[i])
        first[i] = second
        high = second.astype(bf16)
        mirrored = dot_nn(mir_v[...], high).astype(bf16)
        span = slice(i * LINE, (i + 1) * LINE)
        spec_v[0, :half, span] = high[:half]
        spec_v[0, half:, span] = mirrored[:half]
        spec_v[1, :half, span] = jnp.where(top, 0.0, second[half:]).astype(bf16)
        spec_v[1, half:, span] = mirrored[half:]

    mine = pl.multiple_of(spot * width, width)

    def exchange3(d, begin):
        theirs = pl.multiple_of((me ^ d) * steps, steps)
        return pltpu.make_async_remote_copy(
            src_ref=spec_v.at[:, pl.ds(theirs, steps), :],
            dst_ref=spec_out.at[:, :, pl.ds(begin, width)],
            send_sem=send3.at[d], recv_sem=recv3.at[d],
            device_id={"tm": me ^ d, "space": plane}, device_id_type=MESH,
        )

    def exchange4(d, begin):
        theirs = pl.multiple_of((me ^ d) * steps, steps)
        return pltpu.make_async_remote_copy(
            src_ref=time_v.at[pl.ds(theirs, steps), :],
            dst_ref=time_out.at[:, pl.ds(begin, width)],
            send_sem=send4.at[d], recv_sem=recv4.at[d],
            device_id={"tm": me ^ d, "space": plane}, device_id_type=MESH,
        )

    for d in range(tm - 1, 0, -1):
        exchange3(d, mine).start()
    own_spec = pltpu.make_async_copy(
        spec_v.at[:, pl.ds(row, steps), :], spec_out.at[:, :, pl.ds(mine, width)], own_sem.at[0]
    )
    own_spec.start()
    for i in range(lines):
        second = first[i]
        high = second.astype(bf16)
        low = (second - high.astype(jnp.float32)).astype(bf16)
        value = dot_nn(inv_v[0], high) + dot_nn(inv_v[1], high) + dot_nn(inv_v[0], low)
        time_v[:, i * LINE:(i + 1) * LINE] = value.astype(bf16)
    for d in range(tm - 1, 0, -1):
        exchange4(d, mine).start()
    own_time = pltpu.make_async_copy(
        time_v.at[pl.ds(row, steps), :], time_out.at[:, pl.ds(mine, width)], own_sem.at[1]
    )
    own_time.start()

    for d in range(1, tm):
        exchange1(d).wait_send()
    for hop in hops:
        @pl.when(jnp.logical_and(order + hop >= 0, order + hop < total))
        def _():
            for i in range(lines):
                halo(hop, i, order + hop).wait_send()
    own_spec.wait()
    own_time.wait()
    for d in range(1, tm):
        theirs = pl.multiple_of(place(me ^ d, tm) * width, width)
        exchange3(d, theirs).wait_recv()
        exchange4(d, theirs).wait_recv()
        exchange3(d, mine).wait_send()
        exchange4(d, mine).wait_send()


def per_device(tm, space, forcing, op_main, op_mass, jacobi_inv):
    steps, dofs = forcing.shape
    length = steps * tm
    half = length // 2
    lines = dofs // tm // LINE
    width = lines * LINE
    blocks = lines * BX
    held = op_main.shape[0]
    halos = 2 * (BY // lines) * lines
    bf16, f32 = jnp.bfloat16, jnp.float32
    forward, inverse, mirror, coefs = tables(length)
    any_space = pl.BlockSpec(memory_space=pl.ANY)
    vmem = pl.BlockSpec(memory_space=pltpu.VMEM)
    dma = pltpu.SemaphoreType.DMA
    spec, field = pl.pallas_call(
        functools.partial(kernel, tm, space, lines),
        out_shape=(
            jax.ShapeDtypeStruct((2, steps, dofs), bf16),
            jax.ShapeDtypeStruct((steps, dofs), bf16),
        ),
        in_specs=[any_space] * 7 + [vmem],
        out_specs=(any_space, any_space),
        scratch_shapes=[
            pltpu.VMEM((tm, steps, width), f32),
            pltpu.VMEM((tm, steps, width), bf16),
            pltpu.VMEM((length, width), bf16),
            pltpu.VMEM((BS, 7 * BS, held), bf16),
            pltpu.VMEM((BS, 7 * BS, held), bf16),
            pltpu.VMEM((BS, BS, held), bf16),
            pltpu.VMEM((4, blocks * 8, 2 * held), bf16),
            pltpu.VMEM((blocks, BS, 7 * BS), f32),
            pltpu.VMEM((blocks, BS, BS), f32),
            pltpu.VMEM((2, length, length), bf16),
            pltpu.VMEM((2, length, length), bf16),
            pltpu.VMEM((length, length), bf16),
            pltpu.VMEM((lines, 5, 2 * LINE, LINE), bf16),
            pltpu.VMEM((lines, LINE, LINE), bf16),
            pltpu.VMEM((lines + 2 * BY, length, LINE), bf16),
            pltpu.VMEM((lines, length, LINE), f32),
            pltpu.VMEM((lines, length, LINE), f32),
            pltpu.VMEM((lines, length, 2 * LINE), f32),
            pltpu.VMEM((2, length, width), bf16),
            pltpu.VMEM((length, width), bf16),
            dma((3,)), dma((BS // 8,)), dma((BS // 8,)), dma((BS // 8,)), dma((tm,)), dma((2,)),
            dma((tm,)), dma((tm,)),
            dma((halos,)), dma((halos,)),
            dma((tm,)), dma((tm,)),
            dma((tm,)), dma((tm,)),
        ],
        compiler_params=pltpu.CompilerParams(
            collective_id=0, has_side_effects=True, vmem_limit_bytes=56 * 1024 * 1024
        ),
    )(
        forcing, *(jnp.transpose(op, (1, 2, 0)) for op in (op_main, op_mass, jacobi_inv)),
        jnp.asarray(forward), jnp.asarray(inverse), jnp.asarray(mirror), jnp.asarray(coefs),
    )
    return spec[0].astype(f32), spec[1].astype(f32), field.astype(f32)


def solution(mesh):
    in_specs = (
        P("tm", "space"),
        P("space", None, None),
        P("space", None, None),
        P("space", None, None),
    )
    out_specs = (P("tm", "space"), P("tm", "space"), P("tm", "space"))
    body = functools.partial(per_device, mesh.shape["tm"], mesh.shape["space"])
    return jax.shard_map(
        body, mesh=mesh, in_specs=in_specs, out_specs=out_specs, check_vma=False
    )
```

profile of v0, /device:TPU:0, one launch (start us, length us, event | category | flops | bytes accessed | tf_op | source)
XLA Modules:
  0.0 48.6 jit_solution(17933198587803256299)
XLA Ops:
  0.6 43.2 %shard_map.103 = (bf16[2,32,8192]{2,1,0:T(8,128)(2,1)}, bf16[32,8192]{1,0:T(8,128)(2,1)}) custom-call(f32[32,8192]{1,0:T(8,128)} %forcing.1, bf16[64,448,128]{2,1,0:T(8,128)(2,1)} %bitcast.9, bf16[64,448,128]{2,1,0:T(8,128)(2,1)} %bitcast.10, bf16[64,64,128]{2,1,0:T(8,128)(2,1)} %bitcast.11, bf16[2,256,256]{2,1,0:T(8,128)(2,1)} %constant.8.clone.fwd, ...), custom_call_target="tpu_custom_call" | custom-call | tf_op jit(solution)/shard_map/pallas_call | solution.py:375
  43.9 2.7 %bitcast_convert_fusion = (f32[32,8192]{1,0:T(8,128)}, f32[32,8192]{1,0:T(8,128)}) fusion(bf16[2,32,8192]{2,1,0:T(8,128)(2,1)} %get-tuple-element.5), kind=kLoop, calls=%fused_computation | loop fusion | flops 524288 | bytes 3145728 | tf_op jit(solution)/shard_map/convert_element_type | solution.py:417
  46.5 2.1 %convert_element_type.19 = f32[32,8192]{1,0:T(8,128)} convert(bf16[32,8192]{1,0:T(8,128)(2,1)} %get-tuple-element.6) | non-fusion elementwise | flops 262144 | bytes 1572864 | tf_op jit(solution)/shard_map/convert_element_type | solution.py:417
where the time goes:
time: 48.8 us; the launch traced here: 48.6 us
  Pallas kernels  43.2 us (89%)
  other arithmetic  4.73 us (10%)
  between operations  0.64 us (1%)
    pallas_call x1, Pallas kernels, per_device(): pl.pallas_call(functools.partial(kernel, tm, space, lines), out_shape=(ja...  43.2 us
    convert_element_type x2, other arithmetic, per_device(): return (spec[0].astype(f32), spec[1].astype(f32), field.astype(f32))  4.73 us

commit v1 on v0

--- a/solution.py
+++ b/solution.py
@@ -75,11 +75,11 @@
 def kernel(
     tm, space, lines,
     forcing, op_main, op_mass, jacobi, fwd, inv, mir, coef,
-    spec_out, time_out,
+    out,
     wide, sends, cols, main_raw, mass_raw, jac_raw, pick, picked, picked_jac, fwd_v, inv_v, mir_v, weights, gains,
-    field, rhs, first, acc, spec_v, time_v,
+    field, rhs, first, acc, out_v,
     load_sem, main_sem, mass_sem, jac_sem, chunk_sem, own_sem,
-    send1, recv1, send2, recv2, send3, recv3, send4, recv4,
+    send1, recv1, send2, recv2, send3, recv3,
 ):
     bf16 = jnp.bfloat16
     me = lax.axis_index("tm")
@@ -135,35 +135,26 @@
         @pl.when(jnp.logical_and(order + hop >= 0, order + hop < total))
         def _():
             pl.semaphore_signal(barrier, 1, device_id=coords(order + hop), device_id_type=MESH)
-    others = sum(
-        jnp.where(jnp.logical_and(order + hop >= 0, order + hop < total), 1, 0) for hop in hops
-    )
-    pl.semaphore_wait(barrier, tm - 1 + others)
-
     row = pl.multiple_of(me * steps, steps)
 
-    def exchange1(d):
+    def exchange1(i, d, begin):
         return pltpu.make_async_remote_copy(
-            src_ref=sends.at[d], dst_ref=cols.at[pl.ds(row, steps), :],
-            send_sem=send1.at[d], recv_sem=recv1.at[d],
+            src_ref=sends.at[i, d], dst_ref=cols.at[i, pl.ds(begin, steps), :],
+            send_sem=send1.at[i * tm + d], recv_sem=recv1.at[i * tm + d],
             device_id={"tm": me ^ d, "space": plane}, device_id_type=MESH,
         )
 
-    def arrival1(d):
-        theirs = pl.multiple_of((me ^ d) * steps, steps)
-        return pltpu.make_async_remote_copy(
-            src_ref=sends.at[d], dst_ref=cols.at[pl.ds(theirs, steps), :],
-            send_sem=send1.at[d], recv_sem=recv1.at[d],
-            device_id={"tm": me ^ d, "space": plane}, device_id_type=MESH,
-        )
+    def arrival1(i, d):
+        return exchange1(i, d, pl.multiple_of((me ^ d) * steps, steps))
 
     for d, copy in zip(peers, chunks):
         copy.wait()
-        if d == 0:
-            cols[pl.ds(row, steps), :] = wide[d].astype(bf16)
-        else:
-            sends[d] = wide[d].astype(bf16)
-            exchange1(d).start()
+        for i in range(lines):
+            part = wide[d, :, i * LINE:(i + 1) * LINE].astype(bf16)
+            if d == 0:
+                cols[i, pl.ds(row, steps), :] = part
+            else:
+                sends[i, d] = part
 
     held = op_main.shape[2]
     pick_row = lax.broadcasted_iota(jnp.int32, (blocks * 8, 2 * held), 0)
@@ -174,8 +165,8 @@
         hit = jnp.logical_and(same, pick_row % 8 == 2 * p + late)
         pick[p] = jnp.where(hit, 1.0, 0.0).astype(bf16)
 
-    def gather(source, raw, sem, target):
-        @pl.loop(0, groups)
+    def gather(source, raw, sem, target, start, stop):
+        @pl.loop(start, stop)
         def _(g):
             fetch(source, raw, sem, g).wait()
             value = None
@@ -185,6 +176,20 @@
                 value = term if value is None else value + term
             span = pl.ds(pl.multiple_of(g * 8, 8), 8)
             target[:, span, :] = value.reshape(blocks, 8, value.shape[1])
+
+    for hop in hops:
+        @pl.when(jnp.logical_or(order - hop < 0, order - hop >= total))
+        def _():
+            field[pl.ds(BY - hop * lines, lines)] = jnp.zeros((lines, length, LINE), bf16)
+
+    others = sum(
+        jnp.where(jnp.logical_and(order + hop >= 0, order + hop < total), 1, 0) for hop in hops
+    )
+    pl.semaphore_wait(barrier, tm - 1 + others)
+
+    for i in range(lines):
+        for d in peers[:-1]:
+            exchange1(i, d, row).start()
 
     zero = jnp.zeros((BS, BS), bf16)
     first_y = lax.rem(spot * lines, BY)
@@ -209,20 +214,13 @@
                         [piece if j == x else zero for j in range(BX)], axis=1
                     )
 
-    gather(jacobi, jac_raw, jac_sem, picked_jac)
+    gather(jacobi, jac_raw, jac_sem, picked_jac, 0, groups)
     for i in range(lines):
         for x in range(BX):
             own = picked_jac[i * BX + x].astype(bf16)
             gains[i, pl.ds(x * BS, BS), :] = jnp.concatenate(
                 [own if j == x else zero for j in range(BX)], axis=1
             )
-    gather(op_main, main_raw, main_sem, picked)
-    assemble(0)
-
-    for hop in hops:
-        @pl.when(jnp.logical_or(order - hop < 0, order - hop >= total))
-        def _():
-            field[pl.ds(BY - hop * lines, lines)] = jnp.zeros((lines, length, LINE), bf16)
 
     def halo(hop, i, target):
         index = hops.index(hop) * lines + i
@@ -233,11 +231,11 @@
         )
 
     loads[0].wait()
-    for d in range(1, tm):
-        arrival1(d).wait_recv()
-
-    for i in range(lines):
-        part = cols[:, i * LINE:(i + 1) * LINE]
+    for i in range(lines):
+        gather(op_main, main_raw, main_sem, picked, i * groups // lines, (i + 1) * groups // lines)
+        for d in peers[:-1]:
+            arrival1(i, d).wait_recv()
+        part = cols[i]
         hat = dot_nn(fwd_v[0], part) + dot_nn(fwd_v[1], part)
         rhs[i] = hat
         image = dot_nt(hat.astype(bf16), gains[i])
@@ -248,7 +246,8 @@
             def _():
                 halo(hop, i, order + hop).start()
 
-    gather(op_mass, mass_raw, mass_sem, picked)
+    assemble(0)
+    gather(op_mass, mass_raw, mass_sem, picked, 0, groups)
     assemble(1)
 
     def outside(j):
@@ -276,7 +275,17 @@
     own_low = coef[0][:, :1]
     own_high = coef[1][:, :1]
     cross = coef[2][:, :1]
-    seconds = []
+    mine = spot * lines
+
+    def exchange3(i, d, begin):
+        theirs = pl.multiple_of((me ^ d) * steps, steps)
+        return pltpu.make_async_remote_copy(
+            src_ref=out_v.at[i, :, pl.ds(theirs, steps), :], dst_ref=out.at[begin + i],
+            send_sem=send3.at[i * tm + d], recv_sem=recv3.at[i * tm + d],
+            device_id={"tm": me ^ d, "space": plane}, device_id_type=MESH,
+        )
+
+    keep = []
     for i in range(lines):
         if lines == BY:
             arrive(1, i)
@@ -293,75 +302,49 @@
         res_im = rhs[i, half:] - value[half:, :LINE] + own_high * mass_im + cross * mass_re
         residue = jnp.concatenate([res_re.astype(bf16), res_im.astype(bf16)], axis=0)
         second = first[i] + dot_nt(residue, gains[i])
-        first[i] = second
-        high = second.astype(bf16)
-        mirrored = dot_nn(mir_v[...], high).astype(bf16)
-        span = slice(i * LINE, (i + 1) * LINE)
-        spec_v[0, :half, span] = high[:half]
-        spec_v[0, half:, span] = mirrored[:half]
-        spec_v[1, :half, span] = jnp.where(top, 0.0, second[half:]).astype(bf16)
-        spec_v[1, half:, span] = mirrored[half:]
-
-    mine = pl.multiple_of(spot * width, width)
-
-    def exchange3(d, begin):
-        theirs = pl.multiple_of((me ^ d) * steps, steps)
-        return pltpu.make_async_remote_copy(
-            src_ref=spec_v.at[:, pl.ds(theirs, steps), :],
-            dst_ref=spec_out.at[:, :, pl.ds(begin, width)],
-            send_sem=send3.at[d], recv_sem=recv3.at[d],
-            device_id={"tm": me ^ d, "space": plane}, device_id_type=MESH,
-        )
-
-    def exchange4(d, begin):
-        theirs = pl.multiple_of((me ^ d) * steps, steps)
-        return pltpu.make_async_remote_copy(
-            src_ref=time_v.at[pl.ds(theirs, steps), :],
-            dst_ref=time_out.at[:, pl.ds(begin, width)],
-            send_sem=send4.at[d], recv_sem=recv4.at[d],
-            device_id={"tm": me ^ d, "space": plane}, device_id_type=MESH,
-        )
-
-    for d in range(tm - 1, 0, -1):
-        exchange3(d, mine).start()
-    own_spec = pltpu.make_async_copy(
-        spec_v.at[:, pl.ds(row, steps), :], spec_out.at[:, :, pl.ds(mine, width)], own_sem.at[0]
-    )
-    own_spec.start()
-    for i in range(lines):
-        second = first[i]
         high = second.astype(bf16)
         low = (second - high.astype(jnp.float32)).astype(bf16)
+        mirrored = dot_nn(mir_v[...], high).astype(bf16)
+        out_v[i, 0, :half] = high[:half]
+        out_v[i, 0, half:] = mirrored[:half]
+        out_v[i, 1, :half] = jnp.where(top, 0.0, second[half:]).astype(bf16)
+        out_v[i, 1, half:] = mirrored[half:]
         value = dot_nn(inv_v[0], high) + dot_nn(inv_v[1], high) + dot_nn(inv_v[0], low)
-        time_v[:, i * LINE:(i + 1) * LINE] = value.astype(bf16)
-    for d in range(tm - 1, 0, -1):
-        exchange4(d, mine).start()
-    own_time = pltpu.make_async_copy(
-        time_v.at[pl.ds(row, steps), :], time_out.at[:, pl.ds(mine, width)], own_sem.at[1]
-    )
-    own_time.start()
-
-    for d in range(1, tm):
-        exchange1(d).wait_send()
+        out_v[i, 2] = value.astype(bf16)
+        for d in peers[:-1]:
+            exchange3(i, d, mine).start()
+        copy = pltpu.make_async_copy(
+            out_v.at[i, :, pl.ds(row, steps), :], out.at[mine + i], own_sem.at[i]
+        )
+        copy.start()
+        keep.append(copy)
+
+    for i in range(lines):
+        for d in peers[:-1]:
+            exchange1(i, d, row).wait_send()
     for hop in hops:
         @pl.when(jnp.logical_and(order + hop >= 0, order + hop < total))
         def _():
             for i in range(lines):
                 halo(hop, i, order + hop).wait_send()
-    own_spec.wait()
-    own_time.wait()
-    for d in range(1, tm):
-        theirs = pl.multiple_of(place(me ^ d, tm) * width, width)
-        exchange3(d, theirs).wait_recv()
-        exchange4(d, theirs).wait_recv()
-        exchange3(d, mine).wait_send()
-        exchange4(d, mine).wait_send()
+    for i in range(lines):
+        keep[i].wait()
+        for d in peers[:-1]:
+            exchange3(i, d, mine).wait_send()
+            exchange3(i, d, place(me ^ d, tm) * lines).wait_recv()
+
+
+def widen(packed, real, imag, field):
+    for i in range(packed.shape[0]):
+        span = slice(i * LINE, (i + 1) * LINE)
+        real[:, span] = packed[i, 0].astype(jnp.float32)
+        imag[:, span] = packed[i, 1].astype(jnp.float32)
+        field[:, span] = packed[i, 2].astype(jnp.float32)
 
 
 def per_device(tm, space, forcing, op_main, op_mass, jacobi_inv):
     steps, dofs = forcing.shape
     length = steps * tm
-    half = length // 2
     lines = dofs // tm // LINE
     width = lines * LINE
     blocks = lines * BX
@@ -372,18 +355,15 @@
     any_space = pl.BlockSpec(memory_space=pl.ANY)
     vmem = pl.BlockSpec(memory_space=pltpu.VMEM)
     dma = pltpu.SemaphoreType.DMA
-    spec, field = pl.pallas_call(
+    packed = pl.pallas_call(
         functools.partial(kernel, tm, space, lines),
-        out_shape=(
-            jax.ShapeDtypeStruct((2, steps, dofs), bf16),
-            jax.ShapeDtypeStruct((steps, dofs), bf16),
-        ),
+        out_shape=jax.ShapeDtypeStruct((dofs // LINE, 3, steps, LINE), bf16),
         in_specs=[any_space] * 7 + [vmem],
-        out_specs=(any_space, any_space),
+        out_specs=any_space,
         scratch_shapes=[
             pltpu.VMEM((tm, steps, width), f32),
-            pltpu.VMEM((tm, steps, width), bf16),
-            pltpu.VMEM((length, width), bf16),
+            pltpu.VMEM((lines, tm, steps, LINE), bf16),
+            pltpu.VMEM((lines, length, LINE), bf16),
             pltpu.VMEM((BS, 7 * BS, held), bf16),
             pltpu.VMEM((BS, 7 * BS, held), bf16),
             pltpu.VMEM((BS, BS, held), bf16),
@@ -399,13 +379,11 @@
             pltpu.VMEM((lines, length, LINE), f32),
             pltpu.VMEM((lines, length, LINE), f32),
             pltpu.VMEM((lines, length, 2 * LINE), f32),
-            pltpu.VMEM((2, length, width), bf16),
-            pltpu.VMEM((length, width), bf16),
-            dma((3,)), dma((BS // 8,)), dma((BS // 8,)), dma((BS // 8,)), dma((tm,)), dma((2,)),
-            dma((tm,)), dma((tm,)),
+            pltpu.VMEM((lines, 3, length, LINE), bf16),
+            dma((3,)), dma((BS // 8,)), dma((BS // 8,)), dma((BS // 8,)), dma((tm,)), dma((lines,)),
+            dma((lines * tm,)), dma((lines * tm,)),
             dma((halos,)), dma((halos,)),
-            dma((tm,)), dma((tm,)),
-            dma((tm,)), dma((tm,)),
+            dma((lines * tm,)), dma((lines * tm,)),
         ],
         compiler_params=pltpu.CompilerParams(
             collective_id=0, has_side_effects=True, vmem_limit_bytes=56 * 1024 * 1024
@@ -414,7 +392,15 @@
         forcing, *(jnp.transpose(op, (1, 2, 0)) for op in (op_main, op_mass, jacobi_inv)),
         jnp.asarray(forward), jnp.asarray(inverse), jnp.asarray(mirror), jnp.asarray(coefs),
     )
-    return spec[0].astype(f32), spec[1].astype(f32), field.astype(f32)
+    wide = dofs // 4
+    out_spec = pl.BlockSpec((steps, wide), lambda step: (0, step))
+    return pl.pallas_call(
+        widen,
+        grid=(4,),
+        out_shape=[jax.ShapeDtypeStruct((steps, dofs), f32)] * 3,
+        in_specs=[pl.BlockSpec((wide // LINE, 3, steps, LINE), lambda step: (step, 0, 0, 0))],
+        out_specs=[out_spec] * 3,
+    )(packed)
 
 
 def solution(mesh):

time: 48.8 us -> 47.8 us (0.980)
  other arithmetic: 4.73 us -> 0 us
  Pallas kernels: 43.2 us -> 46.9 us
    convert_element_type x2 -> x0, other arithmetic: 4.73 us -> none  [per_device(): return (spec[0].astype(f32), spec[1].astype(f32), field.astype(f32))]
    pallas_call x1 -> x2, Pallas kernels: 43.2 us -> 46.9 us  [the longest x1 43.1 us: per_device(): pl.pallas_call(functools.partial(kernel, tm, space, lines), out_shape=jax...]
where the time goes in v1:
time: 47.8 us; the launch traced here: 47.5 us
  Pallas kernels  46.9 us (98%)
  between operations  0.64 us (1%)
    pallas_call x1, Pallas kernels, per_device(): pl.pallas_call(functools.partial(kernel, tm, space, lines), out_shape=jax...  43.1 us
    pallas_call x1, Pallas kernels, per_device(): pl.pallas_call(widen, grid=(4,), out_shape=[jax.ShapeDtypeStruct((steps,...  3.84 us

profile of v1, /device:TPU:0, one launch (start us, length us, event | category | flops | bytes accessed | tf_op | source)
XLA Modules:
  0.0 47.5 jit_solution(11032377479841929943)
XLA Ops:
  0.6 43.1 %shard_map.103.packed = bf16[32,3,32,256]{3,2,1,0:T(8,128)(2,1)} custom-call(f32[32,8192]{1,0:T(8,128)} %forcing.1, bf16[64,448,128]{2,1,0:T(8,128)(2,1)} %bitcast.3, bf16[64,448,128]{2,1,0:T(8,128)(2,1)} %bitcast.4, bf16[64,64,128]{2,1,0:T(8,128)(2,1)} %bitcast.5, bf16[2,256,256]{2,1,0:T(8,128)(2,1)} %constant.8.clone.fwd, ...), custom_call_target="tpu_custom_call" | custom-call | tf_op jit(solution)/shard_map/pallas_call | solution.py:358
  43.7 3.8 %shard_map.104 = (f32[32,8192]{1,0:T(8,128)}, f32[32,8192]{1,0:T(8,128)}, f32[32,8192]{1,0:T(8,128)}) custom-call(bf16[32,3,32,256]{3,2,1,0:T(8,128)(2,1)} %shard_map.103.packed), custom_call_target="tpu_custom_call" | custom-call | tf_op jit(solution)/shard_map/pallas_call | solution.py:397

commit v2 on v1

--- a/solution.py
+++ b/solution.py
@@ -157,25 +157,25 @@
                 sends[i, d] = part
 
     held = op_main.shape[2]
-    pick_row = lax.broadcasted_iota(jnp.int32, (blocks * 8, 2 * held), 0)
-    pick_col = lax.broadcasted_iota(jnp.int32, (blocks * 8, 2 * held), 1)
-    late = jnp.where(pick_col >= held, 1, 0)
-    same = pick_col - late * held == spot * blocks + pick_row // 8
-    for p in range(4):
-        hit = jnp.logical_and(same, pick_row % 8 == 2 * p + late)
-        pick[p] = jnp.where(hit, 1.0, 0.0).astype(bf16)
+    pick_row = lax.broadcasted_iota(jnp.int32, (2 * blocks, 2 * held), 0)
+    pick_col = lax.broadcasted_iota(jnp.int32, (2 * blocks, 2 * held), 1)
+    late_row = jnp.where(pick_row >= blocks, 1, 0)
+    late_col = jnp.where(pick_col >= held, 1, 0)
+    wanted = pick_row - late_row * blocks + spot * blocks == pick_col - late_col * held
+    hit = jnp.logical_and(wanted, late_row == late_col)
+    pick[...] = jnp.where(hit, 1.0, 0.0).astype(bf16)
 
     def gather(source, raw, sem, target, start, stop):
         @pl.loop(start, stop)
         def _(g):
             fetch(source, raw, sem, g).wait()
-            value = None
             for p in range(4):
                 pair = jnp.concatenate([raw[g * 8 + 2 * p], raw[g * 8 + 2 * p + 1]], axis=1)
-                term = dot_nt(pick[p], pair)
-                value = term if value is None else value + term
-            span = pl.ds(pl.multiple_of(g * 8, 8), 8)
-            target[:, span, :] = value.reshape(blocks, 8, value.shape[1])
+                span = pl.ds(pl.multiple_of((g * 4 + p) * 2 * blocks, 2 * blocks), 2 * blocks)
+                value = dot_nt(pick[...], pair)
+                for t in range(target.shape[0]):
+                    part = value[:, t * 128:(t + 1) * 128]
+                    target[t, span, :part.shape[1]] = part
 
     for hop in hops:
         @pl.when(jnp.logical_or(order - hop < 0, order - hop >= total))
@@ -198,7 +198,10 @@
         for i in range(lines):
             for x in range(BX):
                 block = i * BX + x
-                slot = [picked[block, :, s * BS:(s + 1) * BS].astype(bf16) for s in range(7)]
+                rows = [
+                    picked[t, pl.ds(block, BS, stride=blocks), :].astype(bf16) for t in range(4)
+                ]
+                slot = [rows[s // 2][:, s % 2 * BS:(s % 2 + 1) * BS] for s in range(7)]
                 span = pl.ds(part * LINE + x * BS, BS)
                 along = {x: slot[0], x - 1: slot[1], x + 1: slot[2]}
                 weights[i, 0, span, :] = jnp.concatenate(
@@ -217,7 +220,7 @@
     gather(jacobi, jac_raw, jac_sem, picked_jac, 0, groups)
     for i in range(lines):
         for x in range(BX):
-            own = picked_jac[i * BX + x].astype(bf16)
+            own = picked_jac[0, pl.ds(i * BX + x, BS, stride=blocks), :].astype(bf16)[:, :BS]
             gains[i, pl.ds(x * BS, BS), :] = jnp.concatenate(
                 [own if j == x else zero for j in range(BX)], axis=1
             )
@@ -367,9 +370,9 @@
             pltpu.VMEM((BS, 7 * BS, held), bf16),
             pltpu.VMEM((BS, 7 * BS, held), bf16),
             pltpu.VMEM((BS, BS, held), bf16),
-            pltpu.VMEM((4, blocks * 8, 2 * held), bf16),
-            pltpu.VMEM((blocks, BS, 7 * BS), f32),
-            pltpu.VMEM((blocks, BS, BS), f32),
+            pltpu.VMEM((2 * blocks, 2 * held), bf16),
+            pltpu.VMEM((4, BS * blocks, 128), f32),
+            pltpu.VMEM((1, BS * blocks, 128), f32),
             pltpu.VMEM((2, length, length), bf16),
             pltpu.VMEM((2, length, length), bf16),
             pltpu.VMEM((length, length), bf16),

time: 47.8 us -> 47.6 us (level)
  no operation moved by 1% of the time
where the time goes in v2:
time: 47.6 us; the launch traced here: 47.4 us
  Pallas kernels  46.7 us (98%)
  between operations  0.64 us (1%)
    pallas_call x1, Pallas kernels, per_device(): pl.pallas_call(functools.partial(kernel, tm, space, lines), out_shape=jax...  42.9 us
    pallas_call x1, Pallas kernels, per_device(): pl.pallas_call(widen, grid=(4,), out_shape=[jax.ShapeDtypeStruct((steps,...  3.84 us

profile of v2, /device:TPU:0, one launch (start us, length us, event | category | flops | bytes accessed | tf_op | source)
XLA Modules:
  0.0 47.4 jit_solution(6873359300687033481)
XLA Ops:
  0.6 42.9 %shard_map.103.packed = bf16[32,3,32,256]{3,2,1,0:T(8,128)(2,1)} custom-call(f32[32,8192]{1,0:T(8,128)} %forcing.1, bf16[64,448,128]{2,1,0:T(8,128)(2,1)} %bitcast.3, bf16[64,448,128]{2,1,0:T(8,128)(2,1)} %bitcast.4, bf16[64,64,128]{2,1,0:T(8,128)(2,1)} %bitcast.5, bf16[2,256,256]{2,1,0:T(8,128)(2,1)} %constant.8.clone.fwd, ...), custom_call_target="tpu_custom_call" | custom-call | tf_op jit(solution)/shard_map/pallas_call | solution.py:361
  43.5 3.8 %shard_map.104 = (f32[32,8192]{1,0:T(8,128)}, f32[32,8192]{1,0:T(8,128)}, f32[32,8192]{1,0:T(8,128)}) custom-call(bf16[32,3,32,256]{3,2,1,0:T(8,128)(2,1)} %shard_map.103.packed), custom_call_target="tpu_custom_call" | custom-call | tf_op jit(solution)/shard_map/pallas_call | solution.py:400

commit v3 on v2

--- a/solution.py
+++ b/solution.py
@@ -395,11 +395,11 @@
         forcing, *(jnp.transpose(op, (1, 2, 0)) for op in (op_main, op_mass, jacobi_inv)),
         jnp.asarray(forward), jnp.asarray(inverse), jnp.asarray(mirror), jnp.asarray(coefs),
     )
-    wide = dofs // 4
+    wide = dofs // 2
     out_spec = pl.BlockSpec((steps, wide), lambda step: (0, step))
     return pl.pallas_call(
         widen,
-        grid=(4,),
+        grid=(2,),
         out_shape=[jax.ShapeDtypeStruct((steps, dofs), f32)] * 3,
         in_specs=[pl.BlockSpec((wide // LINE, 3, steps, LINE), lambda step: (step, 0, 0, 0))],
         out_specs=[out_spec] * 3,

time: 47.6 us -> 46.6 us (0.979)
  Pallas kernels: 46.7 us -> 45.8 us
    pallas_call x1, Pallas kernels: 3.84 us -> 2.87 us  [per_device(): pl.pallas_call(widen, grid=(2,), out_shape=[jax.ShapeDtypeStruct((steps,...]
where the time goes in v3:
time: 46.6 us; the launch traced here: 46.4 us
  Pallas kernels  45.8 us (98%)
  between operations  0.64 us (1%)
    pallas_call x1, Pallas kernels, per_device(): pl.pallas_call(functools.partial(kernel, tm, space, lines), out_shape=jax...  42.9 us
    pallas_call x1, Pallas kernels, per_device(): pl.pallas_call(widen, grid=(2,), out_shape=[jax.ShapeDtypeStruct((steps,...  2.87 us

profile of v3, /device:TPU:0, one launch (start us, length us, event | category | flops | bytes accessed | tf_op | source)
XLA Modules:
  0.0 46.4 jit_solution(11149286726358071755)
XLA Ops:
  0.6 42.9 %shard_map.103.packed = bf16[32,3,32,256]{3,2,1,0:T(8,128)(2,1)} custom-call(f32[32,8192]{1,0:T(8,128)} %forcing.1, bf16[64,448,128]{2,1,0:T(8,128)(2,1)} %bitcast.3, bf16[64,448,128]{2,1,0:T(8,128)(2,1)} %bitcast.4, bf16[64,64,128]{2,1,0:T(8,128)(2,1)} %bitcast.5, bf16[2,256,256]{2,1,0:T(8,128)(2,1)} %constant.8.clone.fwd, ...), custom_call_target="tpu_custom_call" | custom-call | tf_op jit(solution)/shard_map/pallas_call | solution.py:361
  43.5 2.9 %shard_map.104 = (f32[32,8192]{1,0:T(8,128)}, f32[32,8192]{1,0:T(8,128)}, f32[32,8192]{1,0:T(8,128)}) custom-call(bf16[32,3,32,256]{3,2,1,0:T(8,128)(2,1)} %shard_map.103.packed), custom_call_target="tpu_custom_call" | custom-call | tf_op jit(solution)/shard_map/pallas_call | solution.py:400
